TPU v7x, 512 devices: a whole 4x4x16 slice. The times are simulated.
512 devices in a mesh: gx: 16 (over z_lo, core), gy: 32 (over z_hi, y, x).
Axes of the slice: x: 4, y: 4, z: 16 (z_hi: 2, z_lo: 8; z = z_hi * 8 + z_lo), core: 2. Of those that a mesh axis runs over, the one named last changes fastest.
Arguments:
- leaf_raw: float32 [16, 32, 768, 768], P('gx', 'gy'), may hold values from -32 to 80, as said below
- medium_class: int32 [16, 32, 12], P('gx', 'gy'), may hold values from 0 to 7
- wave_table: float32 [8], replicated, may hold values from 1 to 4
- boundary_data: float32 [16, 32, 384, 128], P('gx', 'gy'), may hold values from -6 to 6
Outputs:
- parent_rows: float32 [16, 32, 384, 1536], P('gx', 'gy')
- interface_values: float32 [16, 32, 384, 128], P('gx', 'gy')
Inputs may be any that keep to these rules, and one draw needn't show every extreme that they name: Each tile's block leaf_raw[p, q] is symmetric positive semidefinite.
All inputs are finite; a program needn't handle non-finite values.
Results may differ from a plain program's by a relative error of at most 0.0001.
Values sent between devices are 32-bit elements; how exact they have to be, the bound alone decides.
A program may use at most 64 MiB of HBM per device.

v0:
```python
import jax
import jax.numpy as jnp
from jax import lax
from jax.sharding import PartitionSpec as P

highest = lax.Precision.HIGHEST


def shifted(shard, axis, by):
    size = lax.axis_size(axis)
    return lax.ppermute(shard, axis, [(i, (i + by) % size) for i in range(size)])


def product(left_mat, right_mat):
    return jnp.dot(left_mat, right_mat, precision=highest, preferred_element_type=jnp.float32)


def inner_product(left_mat, right_mat):
    return lax.dot_general(
        left_mat,
        right_mat,
        (((0,), (0,)), ((), ())),
        precision=highest,
        preferred_element_type=jnp.float32,
    )


def lower_solve(factor, right_side):
    return lax.linalg.triangular_solve(factor, right_side, left_side=True, lower=True)


def upper_solve(factor, right_side):
    return lax.linalg.triangular_solve(
        factor, right_side, left_side=True, lower=True, transpose_a=True
    )


def level_outer(matrix, side_len):
    return jnp.concatenate(
        [matrix[:, : 2 * side_len], matrix[:, 3 * side_len : 5 * side_len]], axis=1
    )


def level_inner(matrix, side_len):
    return jnp.concatenate(
        [matrix[:, 2 * side_len : 3 * side_len], matrix[:, 5 * side_len :]], axis=1
    )


def ordered(own_part, other_part, parity, concat_axis):
    lower_part = jnp.where(parity == 0, own_part, other_part)
    upper_part = jnp.where(parity == 0, other_part, own_part)
    return jnp.concatenate([lower_part, upper_part], axis=concat_axis)


def body(leaf_raw, medium_class, wave_table, boundary_data):
    raw_block = leaf_raw[0, 0]
    classes = medium_class[0, 0]
    edge_data = boundary_data[0, 0]
    bound_len = raw_block.shape[0]
    side_len = bound_len // 4
    exterior = 3 * side_len
    half_x = lax.axis_size("gx") // 2
    half_y = lax.axis_size("gy") // 2
    column_parity = lax.axis_index("gx") // half_x
    row_parity = lax.axis_index("gy") // half_y
    onehot = (classes[:, None] == jnp.arange(wave_table.shape[0], dtype=jnp.int32)[None, :]).astype(
        jnp.float32
    )
    per_block = product(onehot, wave_table)
    diagonal = 4.0 + jnp.repeat(per_block, bound_len // classes.shape[0])
    leaf_map = 0.5 * (raw_block + raw_block.T) + jnp.diag(diagonal)
    face_rows = leaf_map[exterior:, :]
    sibling = shifted(face_rows, "gx", half_x)
    factor_one = jnp.linalg.cholesky(face_rows[:, exterior:] + sibling[:, exterior:])
    solved_one = lower_solve(
        factor_one, ordered(face_rows[:, :exterior], sibling[:, :exterior], column_parity, 1)
    )
    own_one = lax.dynamic_slice_in_dim(solved_one, column_parity * exterior, exterior, 1)
    zero_one = jnp.zeros((exterior, exterior), jnp.float32)
    level_rows = ordered(
        leaf_map[:exterior, :exterior], zero_one, column_parity, 1
    ) - inner_product(own_one, solved_one)
    outer_rows = level_rows[: 2 * side_len]
    face_two = level_rows[2 * side_len :]
    pair_face = shifted(face_two, "gx", half_x)
    parent_face = ordered(face_two, pair_face, column_parity, 0)
    cousin_face = shifted(parent_face, "gy", half_y)
    factor_two = jnp.linalg.cholesky(
        level_inner(parent_face, side_len) + level_inner(cousin_face, side_len)
    )
    solved_two = lower_solve(
        factor_two,
        ordered(
            level_outer(parent_face, side_len), level_outer(cousin_face, side_len), row_parity, 1
        ),
    )
    own_two = lax.dynamic_slice_in_dim(
        solved_two, row_parity * (4 * side_len) + column_parity * (2 * side_len), 2 * side_len, 1
    )
    zero_two = jnp.zeros((2 * side_len, 4 * side_len), jnp.float32)
    parent_rows = ordered(
        level_outer(outer_rows, side_len), zero_two, row_parity, 1
    ) - inner_product(own_two, solved_two)
    term_two = product(own_two, edge_data)
    summed_two = term_two + shifted(term_two, "gx", half_x)
    summed_two = summed_two + shifted(summed_two, "gy", half_y)
    gy_values = -upper_solve(factor_two, summed_two)
    own_gy = lax.dynamic_slice_in_dim(gy_values, column_parity * side_len, side_len, 0)
    known_part = jnp.concatenate([edge_data, own_gy], axis=0)
    term_one = product(own_one, known_part)
    summed_one = term_one + shifted(term_one, "gx", half_x)
    gx_values = -upper_solve(factor_one, summed_one)
    interface_values = jnp.concatenate([own_gy, gx_values], axis=0)
    return (parent_rows[None, None], interface_values[None, None])


def solution(mesh):
    return jax.shard_map(
        body,
        mesh=mesh,
        in_specs=(P("gx", "gy", None, None), P("gx", "gy", None), P(), P("gx", "gy", None, None)),
        out_specs=(P("gx", "gy", None, None), P("gx", "gy", None, None)),
        check_vma=False,
    )
```

profile of v0, /device:TPU:98, one launch (start us, length us, event | category | flops | bytes accessed | tf_op | source)
XLA Modules:
  0.0 576.2 jit_solution(14325505027212013342)
XLA Ops:
  2.3 3.1 copy.15
  5.3 2.7 fusion.2
  10.5 9.1 %collective-permute-start = (f32[192,768]{1,0:T(8,128)S(1)}, f32[192,768]{1,0:T(8,128)S(1)}, u32[]{:S(2)}, u32[]{:S(2)}) collective-permute-start(f32[192,768]{1,0:T(8,128)S(1)} %copy.16), channel_id=1, source_target_pairs={{0,256},{32,288},{64,320},{96,352},{128,384},{160,416},{192,448},{... | collective-permute-start | bytes 1769480 | tf_op jit(solution)/shard_map/ppermute | solution.py:11
  20.3 1.8 slice_select_fusion.1
  22.1 46.6 %collective-permute-done = f32[192,768]{1,0:T(8,128)S(1)} collective-permute-done((f32[192,768]{1,0:T(8,128)S(1)}, f32[192,768]{1,0:T(8,128)S(1)}, u32[]{:S(2)}, u32[]{:S(2)}) %collective-permute-start) | collective-permute-done | bytes 589856 | tf_op jit(solution)/shard_map/ppermute | solution.py:11
  72.2 11.7 %cholesky.121 = f32[128,128]{1,0:T(8,128)S(1)} custom-call(f32[128,128]{1,0:T(8,128)S(1)} %copy.19), custom_call_target="Cholesky" | custom-call | tf_op jit(solution)/shard_map/jit(cholesky)/cholesky | solution.py:75
  84.7 10.4 %custom-call.40 = f32[1,128,128]{1,2,0:T(8,128)} custom-call(f32[1,128,128]{2,1,0:T(8,128)S(1)} %get-tuple-element.72), custom_call_target="InvertDiagBlocksLowerTriangular" | custom-call | tf_op jit(solution)/shard_map/jit(cholesky)/cholesky | solution.py:75
  96.5 5.9 %cholesky.247 = f32[64,64]{1,0:T(8,128)S(1)} custom-call(f32[64,64]{1,0:T(8,128)S(1)} %copy.21), custom_call_target="Cholesky" | custom-call | tf_op jit(solution)/shard_map/jit(cholesky)/cholesky | solution.py:75
  104.5 19.9 %custom-call.41 = f32[2,128,128]{1,2,0:T(8,128)S(1)} custom-call(f32[2,128,128]{2,1,0:T(8,128)S(1)} %pad_maximum_fusion.9), custom_call_target="InvertDiagBlocksLowerTriangular" | custom-call | tf_op jit(solution)/shard_map/triangular_solve | solution.py:29
  127.3 3.7 convolution_subtract_fusion
  133.1 8.3 %collective-permute-start.1 = (f32[192,1152]{1,0:T(8,128)S(1)}, f32[192,1152]{1,0:T(8,128)S(1)}, u32[]{:S(2)}, u32[]{:S(2)}) collective-permute-start(f32[192,1152]{1,0:T(8,128)S(1)} %copy.24), channel_id=1, source_target_pairs={{0,256},{32,288},{64,320},{96,352},{128,384},{160,416},{192,448},{... | collective-permute-start | bytes 2654216 | tf_op jit(solution)/shard_map/ppermute | solution.py:11
  141.4 95.9 %collective-permute-done.1 = f32[192,1152]{1,0:T(8,128)S(1)} collective-permute-done((f32[192,1152]{1,0:T(8,128)S(1)}, f32[192,1152]{1,0:T(8,128)S(1)}, u32[]{:S(2)}, u32[]{:S(2)}) %collective-permute-start.1) | collective-permute-done | bytes 884768 | tf_op jit(solution)/shard_map/ppermute | solution.py:11
  242.0 89.9 %collective-permute-start.2 = (f32[384,1152]{0,1:T(8,128)}, f32[384,1152]{0,1:T(8,128)}, u32[]{:S(2)}, u32[]{:S(2)}) collective-permute-start(f32[384,1152]{0,1:T(8,128)} %pad_maximum_fusion), channel_id=1, source_target_pairs={{0,16},{1,17},{2,18},{3,19},{4,20},{5,21},{6,22},{7,23},{8,24},{9,... | collective-permute-start | bytes 5308424 | tf_op jit(solution)/shard_map/ppermute | solution.py:11
  333.5 61.9 %collective-permute-done.2 = f32[384,1152]{0,1:T(8,128)} collective-permute-done((f32[384,1152]{0,1:T(8,128)}, f32[384,1152]{0,1:T(8,128)}, u32[]{:S(2)}, u32[]{:S(2)}) %collective-permute-start.2) | collective-permute-done | bytes 1769504 | tf_op jit(solution)/shard_map/ppermute | solution.py:11
  396.9 11.7 %cholesky.262 = f32[128,128]{1,0:T(8,128)S(1)} custom-call(f32[128,128]{1,0:T(8,128)S(1)} %cholesky.310), custom_call_target="Cholesky" | custom-call | tf_op jit(solution)/shard_map/jit(cholesky)/cholesky | solution.py:89
  409.3 9.8 %custom-call.42 = f32[1,128,128]{1,2,0:T(8,128)S(1)} custom-call(f32[1,128,128]{2,1,0:T(8,128)S(1)} %get-tuple-element.70), custom_call_target="InvertDiagBlocksLowerTriangular" | custom-call | tf_op jit(solution)/shard_map/jit(cholesky)/cholesky | solution.py:89
  419.7 11.7 %cholesky.277 = f32[128,128]{1,0:T(8,128)S(1)} custom-call(f32[128,128]{1,0:T(8,128)S(1)} %cholesky.314), custom_call_target="Cholesky" | custom-call | tf_op jit(solution)/shard_map/jit(cholesky)/cholesky | solution.py:89
  432.1 10.0 %custom-call.43 = f32[1,128,128]{1,2,0:T(8,128)S(1)} custom-call(f32[1,128,128]{2,1,0:T(8,128)S(1)} %get-tuple-element.67), custom_call_target="InvertDiagBlocksLowerTriangular" | custom-call | tf_op jit(solution)/shard_map/jit(cholesky)/cholesky | solution.py:89
  442.6 11.7 %cholesky.296 = f32[128,128]{1,0:T(8,128)S(1)} custom-call(f32[128,128]{1,0:T(8,128)S(1)} %convolution_subtract_fusion.5), custom_call_target="Cholesky" | custom-call | tf_op jit(solution)/shard_map/jit(cholesky)/cholesky | solution.py:89
  456.9 7.6 %while.3 = (s32[]{:T(128)}, f32[384,384]{1,0:T(8,128)S(1)}, s32[3,2]{0,1:T(2,128)S(1)}, f32[3,128,128]{2,1,0:T(8,128)}, s32[]{:T(128)}) while((s32[]{:T(128)}, f32[384,384]{1,0:T(8,128)S(1)}, s32[3,2]{0,1:T(2,128)S(1)}, f32[3,128,128]{2,1,0:T(8,128)}, s32[]{:T(128)}) %tuple.54), condition=%wide.while_cond.1, body=%wide.while_body.1.sunk | while | flops 2 | bytes 132205 | solution.py:29
  457.5 1.9 bitcast_dynamic-update-slice_fusion.2
  460.1 1.9 bitcast_dynamic-update-slice_fusion.2
  462.6 1.9 bitcast_dynamic-update-slice_fusion.2
  464.6 30.3 %custom-call.44 = f32[3,128,128]{1,2,0:T(8,128)S(1)} custom-call(f32[3,128,128]{2,1,0:T(8,128)} %get-tuple-element.17), custom_call_target="InvertDiagBlocksLowerTriangular" | custom-call | tf_op jit(solution)/shard_map/triangular_solve | solution.py:29
  499.7 2.7 convolution_subtract_fusion.2
  505.6 22.0 %collective-permute-start.3 = (f32[384,128]{1,0:T(8,128)}, f32[384,128]{1,0:T(8,128)}, u32[]{:S(2)}, u32[]{:S(2)}) collective-permute-start(f32[384,128]{1,0:T(8,128)} %fusion.25), channel_id=1, source_target_pairs={{0,256},{32,288},{64,320},{96,352},{128,384},{160,416},{192,448},{... | collective-permute-start | bytes 589832 | tf_op jit(solution)/shard_map/ppermute | solution.py:11
  527.6 4.6 collective-permute-done.3
  533.2 6.0 %collective-permute-start.4 = (f32[384,128]{1,0:T(8,128)S(1)}, f32[384,128]{1,0:T(8,128)S(1)}, u32[]{:S(2)}, u32[]{:S(2)}) collective-permute-start(f32[384,128]{1,0:T(8,128)S(1)} %add.120), channel_id=1, source_target_pairs={{0,16},{1,17},{2,18},{3,19},{4,20},{5,21},{6,22},{7,23},{8,24},{9,... | collective-permute-start | bytes 589832 | tf_op jit(solution)/shard_map/ppermute | solution.py:11
  540.8 8.7 %collective-permute-done.4 = f32[384,128]{1,0:T(8,128)S(1)} collective-permute-done((f32[384,128]{1,0:T(8,128)S(1)}, f32[384,128]{1,0:T(8,128)S(1)}, u32[]{:S(2)}, u32[]{:S(2)}) %collective-permute-start.4) | collective-permute-done | bytes 196640 | tf_op jit(solution)/shard_map/ppermute | solution.py:11
  554.0 9.4 %collective-permute-start.5 = (f32[192,128]{1,0:T(8,128)}, f32[192,128]{1,0:T(8,128)S(1)}, u32[]{:S(2)}, u32[]{:S(2)}) collective-permute-start(f32[192,128]{1,0:T(8,128)} %fusion.31), channel_id=1, source_target_pairs={{0,256},{32,288},{64,320},{96,352},{128,384},{160,416},{192,448},{... | collective-permute-start | bytes 294920 | tf_op jit(solution)/shard_map/ppermute | solution.py:11
  563.5 6.4 %fusion = f32[1,1,384,1536]{2,3,1,0:T(8,128)} fusion(f32[384,1536]{1,0:T(8,128)S(1)} %pad_maximum_fusion.1, f32[384,768]{0,1:T(8,128)S(1)} %get-tuple-element.63, f32[384,768]{0,1:T(8,128)S(1)} %get-tuple-element.62, s32[]{:T(128)S(6)} %select_n.106), kind=kOutput, calls=%fused_computation.4 | convolution fusion | flops 2719088640 | bytes 7667716 | tf_op jit(solution)/shard_map/dot_general | solution.py:19
  569.9 3.1 copy.29
  (120 shorter events, 46.5 us)
Async XLA Ops:
  0.6 0.7 copy-start
  10.5 58.2 %collective-permute-start = (f32[192,768]{1,0:T(8,128)S(1)}, f32[192,768]{1,0:T(8,128)S(1)}, u32[]{:S(2)}, u32[]{:S(2)}) collective-permute-start(f32[192,768]{1,0:T(8,128)S(1)} %copy.16), channel_id=1, source_target_pairs={{0,256},{32,288},{64,320},{96,352},{128,384},{160,416},{192,448},{... | collective-permute-start | bytes 1769480 | tf_op jit(solution)/shard_map/ppermute | solution.py:11
  69.8 34.6 %copy-start.13 = (f32[128,64]{1,0:T(8,128)S(1)}, f32[128,64]{1,0:T(8,128)}, u32[]{:S(2)}) copy-start(f32[128,64]{1,0:T(8,128)} %pad_convert_fusion) | copy-start | bytes 98308
  104.4 21.0 %copy-start.10 = (f32[192,192]{1,0:T(8,128)}, f32[192,192]{1,0:T(8,128)S(1)}, u32[]{:S(2)}) copy-start(f32[192,192]{1,0:T(8,128)S(1)} %select_select_fusion.1) | copy-start | bytes 442372
  124.4 2.1 copy-start.11
  125.4 1.9 copy-start.2
  125.4 1.9 copy-start.3
  131.1 1.6 copy-start.1
  133.1 104.2 %collective-permute-start.1 = (f32[192,1152]{1,0:T(8,128)S(1)}, f32[192,1152]{1,0:T(8,128)S(1)}, u32[]{:S(2)}, u32[]{:S(2)}) collective-permute-start(f32[192,1152]{1,0:T(8,128)S(1)} %copy.24), channel_id=1, source_target_pairs={{0,256},{32,288},{64,320},{96,352},{128,384},{160,416},{192,448},{... | collective-permute-start | bytes 2654216 | tf_op jit(solution)/shard_map/ppermute | solution.py:11
  242.0 153.4 %collective-permute-start.2 = (f32[384,1152]{0,1:T(8,128)}, f32[384,1152]{0,1:T(8,128)}, u32[]{:S(2)}, u32[]{:S(2)}) collective-permute-start(f32[384,1152]{0,1:T(8,128)} %pad_maximum_fusion), channel_id=1, source_target_pairs={{0,16},{1,17},{2,18},{3,19},{4,20},{5,21},{6,22},{7,23},{8,24},{9,... | collective-permute-start | bytes 5308424 | tf_op jit(solution)/shard_map/ppermute | solution.py:11
  456.9 39.4 %copy-start.5 = (f32[384,384]{0,1:T(8,128)S(1)}, f32[384,384]{0,1:T(8,128)}, u32[]{:S(2)}) copy-start(f32[384,384]{0,1:T(8,128)} %get-tuple-element.54) | copy-start | bytes 1769476
  456.9 39.4 %copy-start.6 = (f32[384,384]{0,1:T(8,128)S(1)}, f32[384,384]{0,1:T(8,128)}, u32[]{:S(2)}) copy-start(f32[384,384]{0,1:T(8,128)} %get-tuple-element.55) | copy-start | bytes 1769476
  464.6 35.2 %copy-start.4 = (f32[384,384]{1,0:T(8,128)}, f32[384,384]{1,0:T(8,128)S(1)}, u32[]{:S(2)}) copy-start(f32[384,384]{1,0:T(8,128)S(1)} %get-tuple-element.125) | copy-start | bytes 1769476
  494.9 7.5 %copy-start.8 = (f32[3,128,128]{1,2,0:T(8,128)}, f32[3,128,128]{1,2,0:T(8,128)S(1)}, u32[]{:S(2)}) copy-start(f32[3,128,128]{1,2,0:T(8,128)S(1)} %custom-call.44) | copy-start | bytes 589828
  503.3 0.9 copy-start.7
  505.6 26.6 %collective-permute-start.3 = (f32[384,128]{1,0:T(8,128)}, f32[384,128]{1,0:T(8,128)}, u32[]{:S(2)}, u32[]{:S(2)}) collective-permute-start(f32[384,128]{1,0:T(8,128)} %fusion.25), channel_id=1, source_target_pairs={{0,256},{32,288},{64,320},{96,352},{128,384},{160,416},{192,448},{... | collective-permute-start | bytes 589832 | tf_op jit(solution)/shard_map/ppermute | solution.py:11
  533.2 16.3 %collective-permute-start.4 = (f32[384,128]{1,0:T(8,128)S(1)}, f32[384,128]{1,0:T(8,128)S(1)}, u32[]{:S(2)}, u32[]{:S(2)}) collective-permute-start(f32[384,128]{1,0:T(8,128)S(1)} %add.120), channel_id=1, source_target_pairs={{0,16},{1,17},{2,18},{3,19},{4,20},{5,21},{6,22},{7,23},{8,24},{9,... | collective-permute-start | bytes 589832 | tf_op jit(solution)/shard_map/ppermute | solution.py:11
  540.6 8.9 %copy-start.9 = (f32[3,128,128]{1,2,0:T(8,128)S(1)}, f32[3,128,128]{1,2,0:T(8,128)}, u32[]{:S(2)}) copy-start(f32[3,128,128]{1,2,0:T(8,128)} %copy-done.8) | copy-start | bytes 589828
  554.0 18.9 %collective-permute-start.5 = (f32[192,128]{1,0:T(8,128)}, f32[192,128]{1,0:T(8,128)S(1)}, u32[]{:S(2)}, u32[]{:S(2)}) collective-permute-start(f32[192,128]{1,0:T(8,128)} %fusion.31), channel_id=1, source_target_pairs={{0,256},{32,288},{64,320},{96,352},{128,384},{160,416},{192,448},{... | collective-permute-start | bytes 294920 | tf_op jit(solution)/shard_map/ppermute | solution.py:11
  569.8 4.0 copy-start.12
where the time goes:
time: 584 us; the launch traced here: 576 us
  waiting for transfers between devices  218 us (37%)
  other arithmetic  152 us (26%)
  starting transfers between devices  145 us (25%)
  matrix products  29.7 us (5%)
  local copies, waits for them, and re-layouts  27.1 us (5%)
    ppermute x6, waiting for transfers between devices, shifted(): lax.ppermute(shard, axis, [(i, (i + by) % size) for i in range(size)])  218 us
    ppermute x6, starting transfers between devices, shifted(): lax.ppermute(shard, axis, [(i, (i + by) % size) for i in range(size)])  145 us
    another operation x11, other arithmetic, body(): jnp.linalg.cholesky(level_inner(parent_face, side_len) + level_inner(cous...  56.9 us
    another operation x10, other arithmetic, lower_solve(): lax.linalg.triangular_solve(factor, right_side, left_side=True, lower=True)  51.2 us
    another operation x7, other arithmetic, body(): jnp.linalg.cholesky(face_rows[:, exterior:] + sibling[:, exterior:])  29.4 us
  transfers between devices with their start and end apart: 6, of which 5 were waited for; matrix products, arithmetic and copies ran while one was open for 3% of the time, Pallas kernels for 0%

commit v1 on v0

v1 whole, which is shorter than its diff:
```python
import functools

import jax
import jax.numpy as jnp
from jax import lax
from jax.experimental import pallas as pl
from jax.experimental.pallas import tpu as pltpu
from jax.sharding import PartitionSpec as P

highest = lax.Precision.HIGHEST
MESH = pl.DeviceIdType.MESH
T = 128
f32 = jnp.float32


def product(left, right):
    return jnp.dot(left, right, precision=highest, preferred_element_type=f32)


def inner(left, right):
    return lax.dot_general(
        left, right, (((0,), (0,)), ((), ())), precision=highest, preferred_element_type=f32
    )


def invert_tile(ref):
    lane = lax.broadcasted_iota(jnp.int32, (8, T), 1)
    sub = lax.broadcasted_iota(jnp.int32, (8, T), 0)
    wide_lane = lax.broadcasted_iota(jnp.int32, (T, T), 1)

    def step(k, carry):
        start = pl.multiple_of(k * 8, 8)
        panel = ref[pl.ds(start, 8), :]
        for j in range(8):
            column = jnp.broadcast_to(panel[:, j : j + 1], (8, T))
            row = jnp.broadcast_to(panel[j : j + 1, :], (8, T))
            pivot = jnp.broadcast_to(panel[j : j + 1, j : j + 1], (8, T))
            scaled = jnp.where(lane == j, 1.0, row) / pivot
            rest = jnp.where(lane == j, 0.0, panel) - column * scaled
            panel = jnp.where(sub == j, scaled, rest)
        whole = ref[...]
        updated = jnp.where(wide_lane < 8, 0.0, whole)
        for j in range(8):
            updated = updated - whole[:, j : j + 1] * panel[j : j + 1, :]
        ref[...] = pltpu.roll(updated, T - 8, 1)
        ref[pl.ds(start, 8), :] = pltpu.roll(panel, T - 8, 1)
        return carry

    lax.fori_loop(0, T // 8, step, 0)


def kernel(
    cls_ref, wave_ref, raw_hbm, data_hbm, rows_hbm, vals_hbm,
    raw, data, kk, rr, qq, mat, trow, dinv, cc, out, vals,
    load_sem, send_sem, recv_sem, store_sem,
):
    gx, gy = lax.axis_index("gx"), lax.axis_index("gy")
    size_x, size_y = lax.axis_size("gx"), lax.axis_size("gy")
    half_x, half_y = size_x // 2, size_y // 2
    col, row = gx // half_x, gy // half_y
    sib = (lax.rem(gx + half_x, size_x), gy)
    diag = (lax.rem(gx + half_x, size_x), lax.rem(gy + half_y, size_y))

    barrier = pltpu.get_barrier_semaphore()
    for peer in (sib, diag):
        pl.semaphore_signal(barrier, inc=1, device_id=peer, device_id_type=MESH)

    low, high = pl.ds(0, 384), pl.ds(384, 384)
    loads = []
    for i, (r, c) in enumerate(((high, high), (high, low), (low, high), (low, low))):
        copy = pltpu.make_async_copy(raw_hbm.at[r, c], raw.at[r, c], load_sem.at[i])
        copy.start()
        loads.append(copy)
    data_copy = pltpu.make_async_copy(data_hbm, data, load_sem.at[4])
    data_copy.start()

    OWN, SIB, DIA, OPP = 0, 1, 2, 3
    flow = [0]

    def send(src, dst, peer):
        i = flow[0]
        flow[0] += 1
        copy = pltpu.make_async_remote_copy(
            src_ref=src, dst_ref=dst, send_sem=send_sem.at[i], recv_sem=recv_sem.at[i],
            device_id=peer, device_id_type=MESH,
        )
        copy.start()
        return copy

    def krow(tile, i):
        return kk.at[tile, pl.ds(T * i, T), pl.ds(0, T * (i + 1))]

    def half(ref, tile, i):
        return ref.at[tile, pl.ds(192 * i, 192), :]

    iota_r = lax.broadcasted_iota(jnp.int32, (T, T), 0)
    iota_c = lax.broadcasted_iota(jnp.int32, (T, T), 1)

    def diagonal(block):
        first = 4.0 + wave_ref[cls_ref[2 * block]]
        second = 4.0 + wave_ref[cls_ref[2 * block + 1]]
        return jnp.where(iota_r == iota_c, jnp.where(iota_r < 64, first, second), 0.0)

    loads[0].wait()
    for i in range(3):
        for j in range(3):
            block = raw[pl.ds(384 + T * i, T), pl.ds(384 + T * j, T)]
            mirror = raw[pl.ds(384 + T * j, T), pl.ds(384 + T * i, T)]
            summed = 0.5 * (block + mirror.T)
            if i == j:
                summed = summed + diagonal(3 + i)
            kk[OWN, pl.ds(T * i, T), pl.ds(T * j, T)] = summed
    pl.semaphore_wait(barrier, 2)

    copies = []
    k_sib, k_dia = {}, {}
    for i in (2, 1, 0):
        k_sib[i] = send(krow(OWN, i), krow(SIB, i), sib)
    for i in (0, 1, 2):
        k_dia[i] = send(krow(OWN, i), krow(DIA, i), diag)

    loads[1].wait()
    loads[2].wait()
    for i in range(3):
        for j in range(3):
            block = raw[pl.ds(384 + T * i, T), pl.ds(T * j, T)]
            mirror = raw[pl.ds(T * j, T), pl.ds(384 + T * i, T)]
            rr[OWN, pl.ds(T * i, T), pl.ds(T * j, T)] = 0.5 * (block + mirror.T)
    data_copy.wait()
    qq[OWN] = product(rr[OWN], data[...])

    k_sib[2].wait_recv()
    k_opp = {2: send(krow(SIB, 2), krow(OPP, 2), diag)}
    for i in (0, 1):
        k_dia[i].wait_recv()
        k_opp[i] = send(krow(DIA, i), krow(OPP, i), sib)

    r_sib, r_dia, q_sib, q_dia = {}, {}, {}, {}
    for i in (0, 1):
        r_sib[i] = send(half(rr, OWN, i), half(rr, SIB, i), sib)
        r_dia[1 - i] = send(half(rr, OWN, 1 - i), half(rr, DIA, 1 - i), diag)
    for i in (0, 1):
        q_sib[i] = send(half(qq, OWN, i), half(qq, SIB, i), sib)
        q_dia[1 - i] = send(half(qq, OWN, 1 - i), half(qq, DIA, 1 - i), diag)

    k_sib[1].wait_recv()
    k_sib[0].wait_recv()
    k_dia[2].wait_recv()

    def tile_block(tile, i, j):
        if i >= j or tile == OWN:
            return kk[tile, pl.ds(T * i, T), pl.ds(T * j, T)]
        return kk[tile, pl.ds(T * j, T), pl.ds(T * i, T)].T

    for i in range(3):
        for j in range(3):
            row_y = iota_r + T * i < 192
            col_y = iota_c + T * j < 192
            own_block = tile_block(OWN, i, j)
            dia_block = tile_block(DIA, i, j)
            same = row_y == col_y
            yy = jnp.logical_and(row_y, col_y)
            yx = jnp.logical_and(row_y, jnp.logical_not(col_y))
            mat[j, pl.ds(T * i, T), :] = tile_block(SIB, i, j) + jnp.where(
                same, jnp.where(yy, dia_block, own_block), 0.0
            )
            mat[3 + j, pl.ds(384 + T * i, T), :] = jnp.where(
                same, jnp.where(yy, own_block, dia_block), 0.0
            )
            mat[3 + j, pl.ds(T * i, T), :] = jnp.where(
                same, 0.0, jnp.where(yx, dia_block, own_block)
            )
            mat[j, pl.ds(384 + T * i, T), :] = jnp.where(
                same, 0.0, jnp.where(yx, own_block, dia_block)
            )

    def sweep(b, carry):
        start = pl.multiple_of(b * T, T)
        dinv[...] = mat[b, pl.ds(start, T), :]
        invert_tile(dinv)
        inverse = dinv[...]

        def scale(j, c):
            trow[j] = product(inverse, mat[j, pl.ds(start, T), :])
            return c

        lax.fori_loop(0, 6, scale, 0)
        trow[b] = inverse
        column = mat[b]
        mat[b] = jnp.zeros((768, T), f32)

        def update(j, c):
            mat[j] = mat[j] - product(column, trow[j])
            mat[j, pl.ds(start, T), :] = trow[j]
            return c

        lax.fori_loop(0, 6, update, 0)
        return carry

    lax.fori_loop(0, 3, sweep, 0)
    for i in range(3):
        k_opp[i].wait_recv()
    for i in range(3):
        for j in range(3):
            mat[3 + j, pl.ds(384 + T * i, T), :] += tile_block(OPP, i, j)
    lax.fori_loop(3, 6, sweep, 0)

    r_sib[0].wait_recv()
    r_opp = {0: send(half(rr, SIB, 0), half(rr, OPP, 0), diag)}
    r_dia[1].wait_recv()
    r_opp[1] = send(half(rr, DIA, 1), half(rr, OPP, 1), sib)
    q_sib[0].wait_recv()
    q_opp = {0: send(half(qq, SIB, 0), half(qq, OPP, 0), diag)}
    q_dia[1].wait_recv()
    q_opp[1] = send(half(qq, DIA, 1), half(qq, OPP, 1), sib)

    own_rows = jnp.concatenate([rr[OWN, pl.ds(192, 192), :], rr[OWN, pl.ds(0, 192), :]], axis=0)
    for j in range(6):
        cc[j] = inner(own_rows, mat[j, pl.ds(192, 384), :])
    left = iota_c < 64
    left = lax.broadcasted_iota(jnp.int32, (384, T), 1) < 64

    def parts(tile):
        if tile == SIB:
            return cc[0], cc[1], cc[2]
        if tile == OPP:
            return cc[3], cc[4], cc[5]
        if tile == DIA:
            return cc[0], jnp.where(left, cc[1], cc[4]), cc[5]
        return cc[3], jnp.where(left, cc[4], cc[1]), cc[2]

    loads[3].wait()
    for i in range(3):
        for j in range(3):
            block = raw[pl.ds(T * i, T), pl.ds(T * j, T)]
            mirror = raw[pl.ds(T * j, T), pl.ds(T * i, T)]
            summed = 0.5 * (block + mirror.T)
            if i == j:
                summed = summed + diagonal(i)
            out[OWN, pl.ds(T * i, T), pl.ds(T * j, T)] = summed

    place = {
        OWN: 2 * row + col,
        SIB: 2 * row + 1 - col,
        DIA: 2 * (1 - row) + 1 - col,
        OPP: 2 * (1 - row) + col,
    }
    stores = []

    def finish(tile):
        total = None
        for j, part in enumerate(parts(tile)):
            term = product(part, rr[tile, pl.ds(T * j, T), :])
            total = term if total is None else total + term
        if tile == OWN:
            out[OWN] = out[OWN] - total
        else:
            out[tile] = -total
        copy = pltpu.make_async_copy(
            out.at[tile],
            rows_hbm.at[:, pl.ds(pl.multiple_of(place[tile] * 384, T), 384)],
            store_sem.at[tile],
        )
        copy.start()
        stores.append(copy)

    finish(OWN)
    r_sib[1].wait_recv()
    finish(SIB)
    r_dia[0].wait_recv()
    finish(DIA)
    r_opp[0].wait_recv()
    r_opp[1].wait_recv()
    finish(OPP)

    q_sib[1].wait_recv()
    q_dia[0].wait_recv()
    q_opp[0].wait_recv()
    q_opp[1].wait_recv()
    upper = lax.broadcasted_iota(jnp.int32, (384, T), 0) < 192
    first = qq[SIB] + jnp.where(upper, qq[DIA], qq[OWN])
    second = qq[OPP] + jnp.where(upper, qq[OWN], qq[DIA])
    total = None
    for j in range(6):
        side = first if j < 3 else second
        term = product(mat[j, pl.ds(192, 384), :], side[T * (j % 3) : T * (j % 3 + 1), :])
        total = term if total is None else total + term
    vals[pl.ds(0, 192), :] = -total[192:, :]
    vals[pl.ds(192, 192), :] = -total[:192, :]
    copy = pltpu.make_async_copy(vals, vals_hbm, store_sem.at[4])
    copy.start()
    stores.append(copy)

    for group in (k_sib, k_dia, k_opp, r_sib, r_dia, r_opp, q_sib, q_dia, q_opp):
        for i in group:
            group[i].wait_send()
    for copy in stores:
        copy.wait()


def body(leaf_raw, medium_class, wave_table, boundary_data):
    raw = leaf_raw[0, 0]
    data = boundary_data[0, 0]
    flows = 6 + 3 + 8 + 4
    rows, vals = pl.pallas_call(
        kernel,
        out_shape=(
            jax.ShapeDtypeStruct((384, 1536), f32),
            jax.ShapeDtypeStruct((384, T), f32),
        ),
        in_specs=[
            pl.BlockSpec(memory_space=pltpu.SMEM),
            pl.BlockSpec(memory_space=pltpu.SMEM),
            pl.BlockSpec(memory_space=pl.ANY),
            pl.BlockSpec(memory_space=pl.ANY),
        ],
        out_specs=(
            pl.BlockSpec(memory_space=pl.ANY),
            pl.BlockSpec(memory_space=pl.ANY),
        ),
        scratch_shapes=[
            pltpu.VMEM((768, 768), f32),
            pltpu.VMEM((384, T), f32),
            pltpu.VMEM((4, 384, 384), f32),
            pltpu.VMEM((4, 384, 384), f32),
            pltpu.VMEM((4, 384, T), f32),
            pltpu.VMEM((6, 768, T), f32),
            pltpu.VMEM((6, T, T), f32),
            pltpu.VMEM((T, T), f32),
            pltpu.VMEM((6, 384, T), f32),
            pltpu.VMEM((4, 384, 384), f32),
            pltpu.VMEM((384, T), f32),
            pltpu.SemaphoreType.DMA((5,)),
            pltpu.SemaphoreType.DMA((flows,)),
            pltpu.SemaphoreType.DMA((flows,)),
            pltpu.SemaphoreType.DMA((5,)),
        ],
        compiler_params=pltpu.CompilerParams(
            collective_id=0, has_side_effects=True, vmem_limit_bytes=48 << 20
        ),
    )(medium_class[0, 0], wave_table, raw, data)
    return rows[None, None], vals[None, None]


def solution(mesh):
    return jax.shard_map(
        body,
        mesh=mesh,
        in_specs=(P("gx", "gy", None, None), P("gx", "gy", None), P(), P("gx", "gy", None, None)),
        out_specs=(P("gx", "gy", None, None), P("gx", "gy", None, None)),
        check_vma=False,
    )
```

time: 584 us -> 248 us (0.42)
  the two profiles are of different devices: /device:TPU:98 before, /device:TPU:44 now
where the time goes in v1:
time: 248 us
  Pallas kernels  242 us (98%)
  local copies, waits for them, and re-layouts  5.98 us (2%)
    pallas_call x1, Pallas kernels, body(): pl.pallas_call(kernel, out_shape=(jax.ShapeDtypeStruct((384, 1536), f32),...  242 us
    unnamed x10, local copies, waits for them, and re-layouts  5.98 us

profile of v1, /device:TPU:44, one launch (start us, length us, event | category | flops | bytes accessed | tf_op | source)
XLA Modules:
  0.0 248.2 jit_solution(16463949101516970600)
XLA Ops:
  0.6 0.0 copy-start
  0.6 1.7 copy-done
  2.3 0.0 copy-start.1
  2.3 0.9 copy-done.1
  3.2 0.0 copy-start.2
  3.2 0.7 copy-done.2
  3.9 0.0 copy-start.3
  3.9 0.7 copy-done.3
  4.5 241.6 %shard_map.59 = (f32[384,1536]{1,0:T(8,128)S(1)}, f32[384,128]{1,0:T(8,128)S(1)}) custom-call(s32[12]{0:T(128)S(1)} %bitcast.9, f32[8]{0:T(128)S(1)} %copy-done.3, f32[768,768]{1,0:T(8,128)S(1)} %bitcast.5, f32[384,128]{1,0:T(8,128)S(1)} %bitcast.7), custom_call_target="tpu_custom_call" | custom-call | tf_op jit(solution)/shard_map/pallas_call | solution.py:305
  246.1 1.4 copy.8
  247.5 0.7 copy.9
Async XLA Ops:
  0.6 1.7 copy-start
  2.3 0.9 copy-start.1
  3.2 0.7 copy-start.2
  3.9 0.7 copy-start.3

commit v2 on v1

v2 whole, which is shorter than its diff:
```python
import functools

import jax
import jax.numpy as jnp
from jax import lax
from jax.experimental import pallas as pl
from jax.experimental.pallas import tpu as pltpu
from jax.sharding import PartitionSpec as P

highest = lax.Precision.HIGHEST
MESH = pl.DeviceIdType.MESH
T = 128
PANEL = 16
SHARE = 32
f32 = jnp.float32


def product(left, right):
    return jnp.dot(left, right, precision=highest, preferred_element_type=f32)


def inner(left, right):
    return lax.dot_general(
        left, right, (((0,), (0,)), ((), ())), precision=highest, preferred_element_type=f32
    )


def invert_tile(ref):
    lane = lax.broadcasted_iota(jnp.int32, (PANEL, T), 1)
    sub = lax.broadcasted_iota(jnp.int32, (PANEL, T), 0)
    wide_lane = lax.broadcasted_iota(jnp.int32, (T, T), 1)

    def spread(block, j):
        return jnp.broadcast_to(block[j : j + 1, :], (PANEL, T))

    def step(k, carry):
        start = pl.multiple_of(k * PANEL, PANEL)
        panel = ref[pl.ds(start, PANEL), :]
        whole = ref[...]
        columns = [jnp.broadcast_to(panel[:, m : m + 1], (PANEL, T)) for m in range(PANEL)]
        for j in range(PANEL):
            column = columns[j]
            inverse = 1.0 / spread(column, j)
            scaled = jnp.where(lane == j, inverse, spread(panel, j) * inverse)
            rest = jnp.where(lane == j, 0.0, panel) - column * scaled
            panel = jnp.where(sub == j, scaled, rest)
            for m in range(j + 1, PANEL):
                pivot_row = spread(columns[m], j) * inverse
                columns[m] = jnp.where(sub == j, pivot_row, columns[m] - column * pivot_row)
        updated = jnp.where(wide_lane < PANEL, 0.0, whole)
        for j in range(PANEL):
            updated = updated - whole[:, j : j + 1] * panel[j : j + 1, :]
        ref[...] = pltpu.roll(updated, T - PANEL, 1)
        ref[pl.ds(start, PANEL), :] = pltpu.roll(panel, T - PANEL, 1)
        return carry

    lax.fori_loop(0, T // PANEL, step, 0)


def kernel(
    cls_ref, wave_ref, raw_hbm, data_hbm, rows_hbm, vals_hbm,
    raw, data, pk, kk, rr, qt, qin, mat, trow, dinv, cc, out, vt, vin, vals,
    load_sem, send_sem, recv_sem, store_sem,
):
    gx, gy = lax.axis_index("gx"), lax.axis_index("gy")
    size_x, size_y = lax.axis_size("gx"), lax.axis_size("gy")
    half_x, half_y = size_x // 2, size_y // 2
    col, row = gx // half_x, gy // half_y
    other_x, other_y = lax.rem(gx + half_x, size_x), lax.rem(gy + half_y, size_y)
    sib, diag, opp = (other_x, gy), (other_x, other_y), (gx, other_y)

    barrier = pltpu.get_barrier_semaphore()
    for peer in (sib, diag, opp):
        pl.semaphore_signal(barrier, inc=1, device_id=peer, device_id_type=MESH)

    low, high = pl.ds(0, 384), pl.ds(384, 384)
    loads = []
    for i, (r, c) in enumerate(((high, high), (high, low), (low, high), (low, low))):
        copy = pltpu.make_async_copy(raw_hbm.at[r, c], raw.at[r, c], load_sem.at[i])
        copy.start()
        loads.append(copy)
    data_copy = pltpu.make_async_copy(data_hbm, data, load_sem.at[4])
    data_copy.start()

    OWN, SIB, DIA, OPP = 0, 1, 2, 3
    place = {
        OWN: 2 * row + col,
        SIB: 2 * row + 1 - col,
        DIA: 2 * (1 - row) + 1 - col,
        OPP: 2 * (1 - row) + col,
    }
    flow = [0]
    sent = []

    def send(src, dst, peer):
        i = flow[0]
        flow[0] += 1
        copy = pltpu.make_async_remote_copy(
            src_ref=src, dst_ref=dst, send_sem=send_sem.at[i], recv_sem=recv_sem.at[i],
            device_id=peer, device_id_type=MESH,
        )
        copy.start()
        sent.append(copy)
        return copy

    def share(tile):
        return pl.ds(pl.multiple_of(place[tile] * SHARE, SHARE), SHARE)

    def khalf(tile, i):
        return pk.at[tile, pl.ds(0, 104) if i == 0 else pl.ds(104, 96), :]

    def rhalf(tile, i):
        return rr.at[tile, pl.ds(192 * i, 192), :]

    iota_r = lax.broadcasted_iota(jnp.int32, (T, T), 0)
    iota_c = lax.broadcasted_iota(jnp.int32, (T, T), 1)
    long_r = lax.broadcasted_iota(jnp.int32, (192, 384), 0)
    long_c = lax.broadcasted_iota(jnp.int32, (192, 384), 1)

    def diagonal(block):
        first = 4.0 + wave_ref[cls_ref[2 * block]]
        second = 4.0 + wave_ref[cls_ref[2 * block + 1]]
        return jnp.where(iota_r == iota_c, jnp.where(iota_r < 64, first, second), 0.0)

    loads[0].wait()
    for i in range(3):
        for j in range(3):
            block = raw[pl.ds(384 + T * i, T), pl.ds(384 + T * j, T)]
            mirror = raw[pl.ds(384 + T * j, T), pl.ds(384 + T * i, T)]
            summed = 0.5 * (block + mirror.T)
            if i == j:
                summed = summed + diagonal(3 + i)
            kk[OWN, pl.ds(T * i, T), pl.ds(T * j, T)] = summed

    shifted = pltpu.roll(kk[OWN, pl.ds(192, 192), :], 192, 1)
    in_y = long_c < 192
    pk[OWN, pl.ds(0, 192), :] = jnp.where(
        jnp.logical_and(in_y, long_c > long_r), shifted, kk[OWN, pl.ds(0, 192), :]
    )
    main = jnp.sum(jnp.where(long_c == long_r, shifted, 0.0), axis=0, keepdims=True)
    pk[OWN, pl.ds(192, 8), :] = jnp.broadcast_to(main, (8, 384))
    pl.semaphore_wait(barrier, 3)

    k_sib, k_dia = {}, {}
    for i in (0, 1):
        k_sib[i] = send(khalf(OWN, i), khalf(SIB, i), sib)
        k_dia[1 - i] = send(khalf(OWN, 1 - i), khalf(DIA, 1 - i), diag)

    loads[1].wait()
    loads[2].wait()
    for i in range(3):
        for j in range(3):
            block = raw[pl.ds(384 + T * i, T), pl.ds(T * j, T)]
            mirror = raw[pl.ds(T * j, T), pl.ds(384 + T * i, T)]
            rr[OWN, pl.ds(T * i, T), pl.ds(T * j, T)] = 0.5 * (block + mirror.T)
    data_copy.wait()
    qt[...] = lax.dot_general(
        data[...].T, rr[OWN], (((1,), (1,)), ((), ())),
        precision=highest, preferred_element_type=f32,
    )

    k_sib[0].wait_recv()
    k_opp = {0: send(khalf(SIB, 0), khalf(OPP, 0), diag)}
    k_dia[1].wait_recv()
    k_opp[1] = send(khalf(DIA, 1), khalf(OPP, 1), sib)

    q_in = [
        send(qt.at[share(OPP), :], qin.at[OPP], opp),
        send(qt.at[share(SIB), :], qin.at[SIB], sib),
        send(qt.at[share(DIA), :], qin.at[DIA], diag),
    ]
    r_sib, r_dia = {}, {}
    for i in (0, 1):
        r_sib[i] = send(rhalf(OWN, i), rhalf(SIB, i), sib)
        r_dia[1 - i] = send(rhalf(OWN, 1 - i), rhalf(DIA, 1 - i), diag)

    def unpack(tile):
        packed = pk[tile, pl.ds(0, 192), :]
        padded = jnp.concatenate([packed[T:, :], jnp.zeros((64, 384), f32)], axis=0)
        turned = []
        for i in range(3):
            lanes = slice(T * i, T * (i + 1))
            turned.append(
                jnp.concatenate(
                    [packed[:T, lanes].T, padded[:, lanes].T, jnp.zeros((T, T), f32)], axis=1
                )
            )
        turned = jnp.concatenate(turned, axis=0)
        top, bottom = turned[:192, :], turned[192:, :]
        kk[tile, pl.ds(0, 192), :] = jnp.where(
            jnp.logical_or(long_c >= 192, long_r >= long_c), packed, top
        )
        xx = jnp.where(
            long_r == long_c,
            jnp.broadcast_to(pk[tile, pl.ds(192, 1), :], (192, 384)),
            jnp.where(long_c > long_r, packed, top),
        )
        kk[tile, pl.ds(192, 192), :] = jnp.where(in_y, bottom, pltpu.roll(xx, 192, 1))

    def kblock(tile, i, j):
        return kk[tile, pl.ds(T * i, T), pl.ds(T * j, T)]

    k_sib[1].wait_recv()
    unpack(SIB)
    k_dia[0].wait_recv()
    unpack(DIA)
    for i in range(3):
        for j in range(3):
            row_y = iota_r + T * i < 192
            col_y = iota_c + T * j < 192
            own_block = kblock(OWN, i, j)
            dia_block = kblock(DIA, i, j)
            same = row_y == col_y
            yy = jnp.logical_and(row_y, col_y)
            yx = jnp.logical_and(row_y, jnp.logical_not(col_y))
            mat[j, pl.ds(T * i, T), :] = kblock(SIB, i, j) + jnp.where(
                same, jnp.where(yy, dia_block, own_block), 0.0
            )
            mat[3 + j, pl.ds(384 + T * i, T), :] = jnp.where(
                same, jnp.where(yy, own_block, dia_block), 0.0
            )
            mat[3 + j, pl.ds(T * i, T), :] = jnp.where(
                same, 0.0, jnp.where(yx, dia_block, own_block)
            )
            mat[j, pl.ds(384 + T * i, T), :] = jnp.where(
                same, 0.0, jnp.where(yx, own_block, dia_block)
            )

    def sweep(b, carry):
        start = pl.multiple_of(b * T, T)
        dinv[...] = mat[b, pl.ds(start, T), :]
        invert_tile(dinv)
        inverse = dinv[...]
        for j in range(6):
            trow[j] = product(inverse, mat[j, pl.ds(start, T), :])
        trow[b] = inverse
        column = mat[b]
        mat[b] = jnp.zeros((768, T), f32)
        for j in range(6):
            mat[j] = mat[j] - product(column, trow[j])
            mat[j, pl.ds(start, T), :] = trow[j]
        return carry

    lax.fori_loop(0, 3, sweep, 0)
    for i in range(2):
        k_opp[i].wait_recv()
    unpack(OPP)
    for i in range(3):
        for j in range(3):
            mat[3 + j, pl.ds(384 + T * i, T), :] += kblock(OPP, i, j)
    lax.fori_loop(3, 6, sweep, 0)

    for copy in q_in:
        copy.wait_recv()
    wide = lax.broadcasted_iota(jnp.int32, (SHARE, 384), 1) < 192
    own_q = qt[share(OWN), :]
    first = qin[SIB] + jnp.where(wide, qin[DIA], own_q)
    second = qin[OPP] + jnp.where(wide, own_q, qin[DIA])
    sides = jnp.concatenate([first, second], axis=1)
    solved = [-product(sides, mat[j]) for j in range(6)]
    near = jnp.concatenate(solved[:3], axis=1)
    far = jnp.concatenate(solved[3:], axis=1)
    vt[SIB] = near
    vt[OPP] = far
    vt[DIA] = jnp.where(wide, near, far)
    vin[share(OWN), :] = jnp.where(wide, far, near)

    r_sib[0].wait_recv()
    r_opp = {0: send(rhalf(SIB, 0), rhalf(OPP, 0), diag)}
    r_dia[1].wait_recv()
    r_opp[1] = send(rhalf(DIA, 1), rhalf(OPP, 1), sib)
    v_in = [
        send(vt.at[OPP], vin.at[share(OWN), :], opp),
        send(vt.at[SIB], vin.at[share(OWN), :], sib),
        send(vt.at[DIA], vin.at[share(OWN), :], diag),
    ]

    own_rows = jnp.concatenate([rr[OWN, pl.ds(192, 192), :], rr[OWN, pl.ds(0, 192), :]], axis=0)
    for j in range(6):
        cc[j] = inner(own_rows, mat[j, pl.ds(192, 384), :])
    left = lax.broadcasted_iota(jnp.int32, (384, T), 1) < 64

    def parts(tile):
        if tile == SIB:
            return cc[0], cc[1], cc[2]
        if tile == OPP:
            return cc[3], cc[4], cc[5]
        if tile == DIA:
            return cc[0], jnp.where(left, cc[1], cc[4]), cc[5]
        return cc[3], jnp.where(left, cc[4], cc[1]), cc[2]

    loads[3].wait()
    for i in range(3):
        for j in range(3):
            block = raw[pl.ds(T * i, T), pl.ds(T * j, T)]
            mirror = raw[pl.ds(T * j, T), pl.ds(T * i, T)]
            summed = 0.5 * (block + mirror.T)
            if i == j:
                summed = summed + diagonal(i)
            out[OWN, pl.ds(T * i, T), pl.ds(T * j, T)] = summed

    stores = []

    def finish(tile):
        total = None
        for j, part in enumerate(parts(tile)):
            term = product(part, rr[tile, pl.ds(T * j, T), :])
            total = term if total is None else total + term
        if tile == OWN:
            out[OWN] = out[OWN] - total
        else:
            out[tile] = -total
        copy = pltpu.make_async_copy(
            out.at[tile],
            rows_hbm.at[:, pl.ds(pl.multiple_of(place[tile] * 384, T), 384)],
            store_sem.at[tile],
        )
        copy.start()
        stores.append(copy)

    finish(OWN)
    r_sib[1].wait_recv()
    finish(SIB)
    r_dia[0].wait_recv()
    finish(DIA)
    r_opp[0].wait_recv()
    r_opp[1].wait_recv()
    finish(OPP)

    for copy in v_in:
        copy.wait_recv()
    vals[...] = vin[...].T
    copy = pltpu.make_async_copy(vals, vals_hbm, store_sem.at[4])
    copy.start()
    stores.append(copy)

    for copy in sent:
        copy.wait_send()
    for copy in stores:
        copy.wait()


def body(leaf_raw, medium_class, wave_table, boundary_data):
    raw = leaf_raw[0, 0]
    data = boundary_data[0, 0]
    flows = 18
    rows, vals = pl.pallas_call(
        kernel,
        out_shape=(
            jax.ShapeDtypeStruct((384, 1536), f32),
            jax.ShapeDtypeStruct((384, T), f32),
        ),
        in_specs=[
            pl.BlockSpec(memory_space=pltpu.SMEM),
            pl.BlockSpec(memory_space=pltpu.SMEM),
            pl.BlockSpec(memory_space=pl.ANY),
            pl.BlockSpec(memory_space=pl.ANY),
        ],
        out_specs=(
            pl.BlockSpec(memory_space=pl.ANY),
            pl.BlockSpec(memory_space=pl.ANY),
        ),
        scratch_shapes=[
            pltpu.VMEM((768, 768), f32),
            pltpu.VMEM((384, T), f32),
            pltpu.VMEM((4, 200, 384), f32),
            pltpu.VMEM((4, 384, 384), f32),
            pltpu.VMEM((4, 384, 384), f32),
            pltpu.VMEM((T, 384), f32),
            pltpu.VMEM((4, SHARE, 384), f32),
            pltpu.VMEM((6, 768, T), f32),
            pltpu.VMEM((6, T, T), f32),
            pltpu.VMEM((T, T), f32),
            pltpu.VMEM((6, 384, T), f32),
            pltpu.VMEM((4, 384, 384), f32),
            pltpu.VMEM((4, SHARE, 384), f32),
            pltpu.VMEM((T, 384), f32),
            pltpu.VMEM((384, T), f32),
            pltpu.SemaphoreType.DMA((5,)),
            pltpu.SemaphoreType.DMA((flows,)),
            pltpu.SemaphoreType.DMA((flows,)),
            pltpu.SemaphoreType.DMA((5,)),
        ],
        compiler_params=pltpu.CompilerParams(
            collective_id=0, has_side_effects=True, vmem_limit_bytes=66 * 1000 * 1000
        ),
    )(medium_class[0, 0], wave_table, raw, data)
    return rows[None, None], vals[None, None]


def solution(mesh):
    return jax.shard_map(
        body,
        mesh=mesh,
        in_specs=(P("gx", "gy", None, None), P("gx", "gy", None), P(), P("gx", "gy", None, None)),
        out_specs=(P("gx", "gy", None, None), P("gx", "gy", None, None)),
        check_vma=False,
    )
```

time: 248 us -> 162 us (0.65)
  the two profiles are of different devices: /device:TPU:44 before, /device:TPU:1 now
where the time goes in v2:
time: 162 us
  Pallas kernels  157 us (97%)
  local copies, waits for them, and re-layouts  3.94 us (2%)
    pallas_call x1, Pallas kernels, body(): pl.pallas_call(kernel, out_shape=(jax.ShapeDtypeStruct((384, 1536), f32),...  157 us
    unnamed x4, local copies, waits for them, and re-layouts  3.94 us

profile of v2, /device:TPU:1, one launch (start us, length us, event | category | flops | bytes accessed | tf_op | source)
XLA Modules:
  0.0 162.0 jit_solution(9018274289791003544)
XLA Ops:
  0.6 157.4 %shard_map.59 = (f32[384,1536]{1,0:T(8,128)}, f32[384,128]{1,0:T(8,128)}) custom-call(s32[12]{0:T(128)} %bitcast.9, f32[8]{0:T(128)} %wave_ref.1, f32[768,768]{1,0:T(8,128)} %bitcast.5, f32[384,128]{1,0:T(8,128)} %bitcast.7), custom_call_target="tpu_custom_call" | custom-call | tf_op jit(solution)/shard_map/pallas_call | solution.py:347
  158.1 0.0 copy-start
  158.1 3.3 %copy.8 = f32[1,1,384,1536]{3,2,1,0:T(8,128)} copy(f32[1,1,384,1536]{3,2,1,0:T(8,128)} %bitcast.6) | data formatting | bytes 4718592
  161.3 0.0 copy-done
  161.3 0.7 copy.9
Async XLA Ops:
  158.1 3.3 %copy-start = (f32[384,128]{1,0:T(8,128)S(1)}, f32[384,128]{1,0:T(8,128)}, u32[]{:S(2)}) copy-start(f32[384,128]{1,0:T(8,128)} %get-tuple-element.5) | copy-start | bytes 589828

commit v3 on v2

--- a/solution.py
+++ b/solution.py
@@ -109,8 +109,8 @@
     def khalf(tile, i):
         return pk.at[tile, pl.ds(0, 104) if i == 0 else pl.ds(104, 96), :]
 
-    def rhalf(tile, i):
-        return rr.at[tile, pl.ds(192 * i, 192), :]
+    def rchunk(tile, start, size):
+        return rr.at[tile, pl.ds(start, size), :]
 
     iota_r = lax.broadcasted_iota(jnp.int32, (T, T), 0)
     iota_c = lax.broadcasted_iota(jnp.int32, (T, T), 1)
@@ -169,10 +169,14 @@
         send(qt.at[share(SIB), :], qin.at[SIB], sib),
         send(qt.at[share(DIA), :], qin.at[DIA], diag),
     ]
-    r_sib, r_dia = {}, {}
-    for i in (0, 1):
-        r_sib[i] = send(rhalf(OWN, i), rhalf(SIB, i), sib)
-        r_dia[1 - i] = send(rhalf(OWN, 1 - i), rhalf(DIA, 1 - i), diag)
+
+    def send_rows(start, size, peer, tile):
+        return send(rchunk(OWN, start, size), rchunk(tile, start, size), peer)
+
+    r_sib = [send_rows(0, T, sib, SIB)]
+    r_dia = [send_rows(256, T, diag, DIA)]
+    r_sib += [send_rows(T, 64, sib, SIB), send_rows(192, 192, sib, SIB)]
+    r_dia += [send_rows(192, 64, diag, DIA), send_rows(0, 192, diag, DIA)]
 
     def unpack(tile):
         packed = pk[tile, pl.ds(0, 192), :]
@@ -250,6 +254,7 @@
             mat[3 + j, pl.ds(384 + T * i, T), :] += kblock(OPP, i, j)
     lax.fori_loop(3, 6, sweep, 0)
 
+
     for copy in q_in:
         copy.wait_recv()
     wide = lax.broadcasted_iota(jnp.int32, (SHARE, 384), 1) < 192
@@ -265,15 +270,20 @@
     vt[DIA] = jnp.where(wide, near, far)
     vin[share(OWN), :] = jnp.where(wide, far, near)
 
-    r_sib[0].wait_recv()
-    r_opp = {0: send(rhalf(SIB, 0), rhalf(OPP, 0), diag)}
-    r_dia[1].wait_recv()
-    r_opp[1] = send(rhalf(DIA, 1), rhalf(OPP, 1), sib)
     v_in = [
         send(vt.at[OPP], vin.at[share(OWN), :], opp),
         send(vt.at[SIB], vin.at[share(OWN), :], sib),
         send(vt.at[DIA], vin.at[share(OWN), :], diag),
     ]
+    r_opp = []
+    r_sib[0].wait_recv()
+    r_opp.append(send(rchunk(SIB, 0, T), rchunk(OPP, 0, T), diag))
+    r_dia[0].wait_recv()
+    r_opp.append(send(rchunk(DIA, 256, T), rchunk(OPP, 256, T), sib))
+    r_sib[1].wait_recv()
+    r_opp.append(send(rchunk(SIB, T, 64), rchunk(OPP, T, 64), diag))
+    r_dia[1].wait_recv()
+    r_opp.append(send(rchunk(DIA, 192, 64), rchunk(OPP, 192, 64), sib))
 
     own_rows = jnp.concatenate([rr[OWN, pl.ds(192, 192), :], rr[OWN, pl.ds(0, 192), :]], axis=0)
     for j in range(6):
@@ -301,15 +311,10 @@
 
     stores = []
 
-    def finish(tile):
-        total = None
-        for j, part in enumerate(parts(tile)):
-            term = product(part, rr[tile, pl.ds(T * j, T), :])
-            total = term if total is None else total + term
-        if tile == OWN:
-            out[OWN] = out[OWN] - total
-        else:
-            out[tile] = -total
+    def term(tile, j):
+        return product(parts(tile)[j], rr[tile, pl.ds(T * j, T), :])
+
+    def store(tile):
         copy = pltpu.make_async_copy(
             out.at[tile],
             rows_hbm.at[:, pl.ds(pl.multiple_of(place[tile] * 384, T), 384)],
@@ -318,15 +323,17 @@
         copy.start()
         stores.append(copy)
 
-    finish(OWN)
-    r_sib[1].wait_recv()
-    finish(SIB)
-    r_dia[0].wait_recv()
-    finish(DIA)
+    out[OWN] = out[OWN] - (term(OWN, 0) + term(OWN, 1) + term(OWN, 2))
+    store(OWN)
+    r_sib[2].wait_recv()
+    out[SIB] = -(term(SIB, 0) + term(SIB, 1) + term(SIB, 2))
+    store(SIB)
+    r_dia[2].wait_recv()
+    out[DIA] = -(term(DIA, 0) + term(DIA, 1) + term(DIA, 2))
+    store(DIA)
     r_opp[0].wait_recv()
     r_opp[1].wait_recv()
-    finish(OPP)
-
+    out[OPP] = -(term(OPP, 0) + term(OPP, 2))
     for copy in v_in:
         copy.wait_recv()
     vals[...] = vin[...].T
@@ -334,6 +341,11 @@
     copy.start()
     stores.append(copy)
 
+    r_opp[2].wait_recv()
+    r_opp[3].wait_recv()
+    out[OPP] = out[OPP] - term(OPP, 1)
+    store(OPP)
+
     for copy in sent:
         copy.wait_send()
     for copy in stores:
@@ -343,7 +355,7 @@
 def body(leaf_raw, medium_class, wave_table, boundary_data):
     raw = leaf_raw[0, 0]
     data = boundary_data[0, 0]
-    flows = 18
+    flows = 22
     rows, vals = pl.pallas_call(
         kernel,
         out_shape=(
@@ -353,8 +365,8 @@
         in_specs=[
             pl.BlockSpec(memory_space=pltpu.SMEM),
             pl.BlockSpec(memory_space=pltpu.SMEM),
-            pl.BlockSpec(memory_space=pl.ANY),
-            pl.BlockSpec(memory_space=pl.ANY),
+            pl.BlockSpec(memory_space=pltpu.HBM),
+            pl.BlockSpec(memory_space=pltpu.HBM),
         ],
         out_specs=(
             pl.BlockSpec(memory_space=pl.ANY),
@@ -382,7 +394,7 @@
             pltpu.SemaphoreType.DMA((5,)),
         ],
         compiler_params=pltpu.CompilerParams(
-            collective_id=0, has_side_effects=True, vmem_limit_bytes=66 * 1000 * 1000
+            collective_id=0, has_side_effects=True, vmem_limit_bytes=48 << 20
         ),
     )(medium_class[0, 0], wave_table, raw, data)
     return rows[None, None], vals[None, None]

time: 162 us -> 165 us (1.019)
  local copies, waits for them, and re-layouts: 3.94 us -> 5.98 us
    unnamed x4 -> x10, local copies, waits for them, and re-layouts: 3.94 us -> 5.98 us
where the time goes in v3:
time: 165 us
  Pallas kernels  158 us (96%)
  local copies, waits for them, and re-layouts  5.98 us (4%)
    pallas_call x1, Pallas kernels, body(): pl.pallas_call(kernel, out_shape=(jax.ShapeDtypeStruct((384, 1536), f32),...  158 us
    unnamed x10, local copies, waits for them, and re-layouts  5.98 us

profile of v3, /device:TPU:1, one launch (start us, length us, event | category | flops | bytes accessed | tf_op | source)
XLA Modules:
  0.0 164.6 jit_solution(14108765307599753604)
XLA Ops:
  0.6 0.0 copy-start
  0.6 1.7 %copy-done = f32[1,1,768,768]{3,2,1,0:T(8,128)S(1)} copy-done((f32[1,1,768,768]{3,2,1,0:T(8,128)S(1)}, f32[1,1,768,768]{3,2,1,0:T(8,128)}, u32[]{:S(2)}) %copy-start) | copy-done | bytes 2359320
  2.3 0.0 copy-start.1
  2.3 0.9 copy-done.1
  3.2 0.0 copy-start.2
  3.2 0.7 copy-done.2
  3.9 0.0 copy-start.3
  3.9 0.7 copy-done.3
  4.5 157.9 %shard_map.59 = (f32[384,1536]{1,0:T(8,128)S(1)}, f32[384,128]{1,0:T(8,128)S(1)}) custom-call(s32[12]{0:T(128)S(1)} %bitcast.9, f32[8]{0:T(128)S(1)} %copy-done.3, f32[768,768]{1,0:T(8,128)S(1)} %bitcast.5, f32[384,128]{1,0:T(8,128)S(1)} %bitcast.7), custom_call_target="tpu_custom_call" | custom-call | tf_op jit(solution)/shard_map/pallas_call | solution.py:359
  162.5 1.4 copy.8
  163.9 0.7 copy.9
Async XLA Ops:
  0.6 1.7 %copy-start = (f32[1,1,768,768]{3,2,1,0:T(8,128)S(1)}, f32[1,1,768,768]{3,2,1,0:T(8,128)}, u32[]{:S(2)}) copy-start(f32[1,1,768,768]{3,2,1,0:T(8,128)} %param.4) | copy-start | bytes 7077892
  2.3 0.9 copy-start.1
  3.2 0.7 copy-start.2
  3.9 0.7 copy-start.3

commit v4 on v3

--- a/solution.py
+++ b/solution.py
@@ -353,8 +353,8 @@
 
 
 def body(leaf_raw, medium_class, wave_table, boundary_data):
-    raw = leaf_raw[0, 0]
-    data = boundary_data[0, 0]
+    raw = pltpu.with_memory_space_constraint(leaf_raw[0, 0], pltpu.HBM)
+    data = pltpu.with_memory_space_constraint(boundary_data[0, 0], pltpu.HBM)
     flows = 22
     rows, vals = pl.pallas_call(
         kernel,
@@ -396,7 +396,11 @@
         compiler_params=pltpu.CompilerParams(
             collective_id=0, has_side_effects=True, vmem_limit_bytes=48 << 20
         ),
-    )(medium_class[0, 0], wave_table, raw, data)
+    )(
+        pltpu.with_memory_space_constraint(medium_class[0, 0], pltpu.HBM),
+        pltpu.with_memory_space_constraint(wave_table, pltpu.HBM),
+        raw, data,
+    )
     return rows[None, None], vals[None, None]
 
 

time: 165 us -> 161 us (0.976)
  local copies, waits for them, and re-layouts: 5.98 us -> 2.08 us
    unnamed x10 -> x2, local copies, waits for them, and re-layouts: 5.98 us -> 2.08 us
where the time goes in v4:
time: 161 us
  Pallas kernels  158 us (98%)
  local copies, waits for them, and re-layouts  2.08 us (1%)
    pallas_call x1, Pallas kernels, body(): pl.pallas_call(kernel, out_shape=(jax.ShapeDtypeStruct((384, 1536), f32),...  158 us

profile of v4, /device:TPU:1, one launch (start us, length us, event | category | flops | bytes accessed | tf_op | source)
XLA Modules:
  0.0 160.7 jit_solution(5502967097175439854)
XLA Ops:
  0.6 158.0 %shard_map.59 = (f32[384,1536]{1,0:T(8,128)S(1)}, f32[384,128]{1,0:T(8,128)S(1)}) custom-call(s32[12]{0:T(128)} %bitcast.9, f32[8]{0:T(128)} %wave_ref.1, f32[768,768]{1,0:T(8,128)} %bitcast.7, f32[384,128]{1,0:T(8,128)} %bitcast.8), custom_call_target="tpu_custom_call" | custom-call | tf_op jit(solution)/shard_map/pallas_call | solution.py:359
  158.6 1.4 copy.8
  160.0 0.7 copy.9
